TPU v7x, 256 devices: a whole 4x4x8 slice. The times are simulated.
256 devices in a mesh: replica: 32 (over x, z_lo, y), fsdp: 8 (over z_hi, core).
Axes of the slice: x: 4, y: 4, z: 8 (z_hi: 4, z_lo: 2; z = z_hi * 2 + z_lo), core: 2. Of those that a mesh axis runs over, the one named last changes fastest.
Arguments:
- tokens: bfloat16 [131072, 4096], P(('replica', 'fsdp')), may hold values from -6 to 6
- key_cotangent: bfloat16 [131072, 512], P(('replica', 'fsdp')), may hold values from -0.1875 to 0.1875
- key_weight: bfloat16 [131072, 512], P(('replica', 'fsdp')), may hold values from -0.09375 to 0.09375
- first_moment: float32 [131072, 512], P(('replica', 'fsdp')), may hold values from -6 to 6
- second_moment: float32 [131072, 512], P(('replica', 'fsdp')), may hold values from 0.1 to 3
- local_slab: bfloat16 [49152, 4096], P(('replica', 'fsdp')), as said below
- outer_params: float32 [1536, 4096], P('fsdp', 'replica')
- outer_momentum: float32 [1536, 4096], P('fsdp', 'replica'), may hold values from -3 to 3
Outputs:
- projected: bfloat16 [131072, 512], P(('replica', 'fsdp'))
- new_weight: bfloat16 [131072, 512], P(('replica', 'fsdp'))
- new_first: float32 [131072, 512], P(('replica', 'fsdp'))
- new_second: float32 [131072, 512], P(('replica', 'fsdp'))
- new_outer: float32 [1536, 4096], P('fsdp', 'replica')
- new_momentum: float32 [1536, 4096], P('fsdp', 'replica')
- new_local: bfloat16 [49152, 4096], P(('replica', 'fsdp'))
Inputs may be any that keep to these rules, and one draw needn't show every extreme that they name: `local_slab`: each replica's fragment equals outer_params plus a drift that the replicas partly share.
All inputs are finite; a program needn't handle non-finite values.
Results may differ from a plain program's by a relative error of at most 0.00045.
Values may be sent and summed in bfloat16 or wider, within the bound.
A program may use at most 128 MiB of HBM per device.

v0:
```python
import jax
import jax.numpy as jnp
from jax import lax
from jax.sharding import PartitionSpec as P

BETA_ONE = 0.9
BETA_TWO = 0.95
INNER_RATE = 0.001
DECAY_RATE = 0.1
EPSILON = 1e-08
FIRST_FIX = 1.0 - (0.9**50) ** 2
SECOND_FIX = 1.0 - (0.95**50) ** 2
OUTER_RATE = 0.7
OUTER_MOMENTUM = 0.9
MERGE_WEIGHT = 0.5


def outer_update(outer_params, outer_momentum, summed, replicas):
    average = summed / replicas
    pseudo_grad = outer_params - average
    new_momentum = OUTER_MOMENTUM * outer_momentum + pseudo_grad
    new_outer = outer_params - OUTER_RATE * (pseudo_grad + OUTER_MOMENTUM * new_momentum)
    return (new_outer, new_momentum)


def shards(
    tokens,
    key_cotangent,
    key_weight,
    first_moment,
    second_moment,
    local_slab,
    outer_params,
    outer_momentum,
):
    columns = tokens
    projected = jnp.dot(
        columns,
        lax.all_gather(key_weight, "fsdp", axis=0, tiled=True),
        preferred_element_type=jnp.float32,
    ).astype(jnp.bfloat16)
    columns = tokens
    gradient = lax.psum_scatter(
        lax.dot_general(
            columns, key_cotangent, (((0,), (0,)), ((), ())), preferred_element_type=jnp.float32
        ),
        "fsdp",
        scatter_dimension=0,
        tiled=True,
    )
    new_first = BETA_ONE * first_moment + (1.0 - BETA_ONE) * gradient
    new_second = BETA_TWO * second_moment + (1.0 - BETA_TWO) * gradient * gradient
    weight_f = key_weight.astype(jnp.float32)
    update = (
        new_first / FIRST_FIX / (jnp.sqrt(new_second / SECOND_FIX) + EPSILON)
        + DECAY_RATE * weight_f
    )
    new_weight = (weight_f - INNER_RATE * update).astype(jnp.bfloat16)
    replicas = lax.axis_size("replica")
    column_count = outer_params.shape[1]
    slab_f = local_slab.astype(jnp.float32)
    whole_params, whole_momentum = (
        lax.all_gather(outer_params, "replica", axis=1, tiled=True),
        lax.all_gather(outer_momentum, "replica", axis=1, tiled=True),
    )
    summed = lax.psum(slab_f, "replica")
    whole_outer, whole_new_momentum = outer_update(whole_params, whole_momentum, summed, replicas)
    first_column = lax.axis_index("replica") * column_count
    new_outer = lax.dynamic_slice_in_dim(whole_outer, first_column, column_count, 1)
    new_momentum = lax.dynamic_slice_in_dim(whole_new_momentum, first_column, column_count, 1)
    new_local = (MERGE_WEIGHT * slab_f + (1.0 - MERGE_WEIGHT) * whole_outer).astype(jnp.bfloat16)
    return (projected, new_weight, new_first, new_second, new_outer, new_momentum, new_local)


def solution(mesh):
    return jax.shard_map(
        shards,
        mesh=mesh,
        in_specs=(
            P(("replica", "fsdp"), None),
            P(("replica", "fsdp"), None),
            P(("replica", "fsdp"), None),
            P(("replica", "fsdp"), None),
            P(("replica", "fsdp"), None),
            P(("replica", "fsdp"), None),
            P("fsdp", "replica"),
            P("fsdp", "replica"),
        ),
        out_specs=(
            P(("replica", "fsdp"), None),
            P(("replica", "fsdp"), None),
            P(("replica", "fsdp"), None),
            P(("replica", "fsdp"), None),
            P("fsdp", "replica"),
            P("fsdp", "replica"),
            P(("replica", "fsdp"), None),
        ),
        check_vma=False,
    )
```

profile of v0, /device:TPU:34, one launch (start us, length us, event | category | flops | bytes accessed | tf_op | source)
XLA Modules:
  0.0 471.2 jit_solution(1939503694912655858)
XLA Ops:
  7.2 0.0 copy-start
  7.2 0.0 all-gather.6.cloned.1.call-start
  7.2 0.7 all-gather.6.cloned.1.call-update
  7.9 0.0 all-gather.8.cloned.1.call-start
  8.0 0.7 all-gather.8.cloned.1.call-update
  8.7 0.0 all-gather.4.cloned.1.call-start
  8.7 0.7 all-gather.4.cloned.1.call-update
  9.4 0.0 reduce-scatter.2.cloned.1.call-start
  9.4 0.0 copy-done
  9.5 7.8 %fusion.5 = f32[4096,512]{1,0:T(8,128)} fusion(bf16[512,4096]{1,0:T(8,128)(2,1)} %param.8, bf16[512,512]{1,0:T(8,128)(2,1)S(1)} %copy-done), kind=kOutput, calls=%fused_computation.15 | convolution fusion | flops 2147483648 | bytes 13107200 | tf_op jit(solution)/shard_map/dot_general | solution.py:44
  17.3 0.0 copy-start.1
  17.3 0.0 reduce-scatter.2.cloned.1.call-update
  17.3 1.4 copy-done.1
  18.7 173.2 %all-reduce.1 = f32[192,4096]{1,0:T(8,128)} all-reduce(bf16[192,4096]{1,0:T(8,128)(2,1)S(1)} %copy-done.1), channel_id=1, replica_groups=mesh['replica'=32,'fsdp'=8] {'replica'}, use_global_device_ids=true, to_apply=%region_1.0 | all-reduce | flops 786432 | bytes 4718592 | tf_op jit(solution)/shard_map/psum | solution.py:66
  191.8 111.6 %all-gather.8.cloned.1.call-done = f32[192,4096]{1,0:T(8,128)} async-done(((f32[192,128]{1,0:T(8,128)}), f32[192,4096]{1,0:T(8,128)}) %all-gather.8.cloned.1.call-update) | async-done | bytes 3145744 | tf_op jit(solution)/shard_map/all_gather | solution.py:64
  303.4 6.2 %multiply_convert_fusion = (bf16[192,4096]{1,0:T(8,128)(2,1)}, f32[192,4096]{1,0:T(8,128)S(1)}, f32[192,4096]{1,0:T(8,128)S(1)}) fusion(bf16[192,4096]{1,0:T(8,128)(2,1)S(1)} %copy-done.1, f32[192,4096]{1,0:T(8,128)} %all-gather.6.cloned.1.call-done, f32[192,4096]{1,0:T(8,128)} %all-gather.8.cloned.1.call-done, f32[192,4096]{1,0:T(8,128)} %all-reduce.1), kind=kLoop, calls=%fused_computation | loop fusion | flops 9437184 | bytes 18874368 | tf_op jit(solution)/shard_map/convert_element_type | solution.py:71
  309.6 0.7 constant_dynamic-slice_fusion
  310.3 51.1 %all-gather.4.cloned.1.call-done = bf16[4096,512]{1,0:T(8,128)(2,1)} async-done(((bf16[512,512]{1,0:T(8,128)(2,1)}), bf16[4096,512]{1,0:T(8,128)(2,1)}) %all-gather.4.cloned.1.call-update) | async-done | bytes 4194320 | tf_op jit(solution)/shard_map/all_gather | solution.py:39
  361.3 6.6 %convolution_convert_fusion = bf16[512,512]{1,0:T(8,128)(2,1)} fusion(bf16[512,4096]{1,0:T(8,128)(2,1)} %param.8, bf16[4096,512]{1,0:T(8,128)(2,1)} %all-gather.4.cloned.1.call-done), kind=kOutput, calls=%fused_computation.7 | convolution fusion | flops 2147745792 | bytes 8912896 | tf_op jit(solution)/shard_map/dot_general | solution.py:37
  367.9 93.3 %reduce-scatter.2.cloned.1.call-done = f32[512,512]{1,0:T(8,128)} async-done(((f32[4096,512]{1,0:T(8,128)}), f32[512,512]{1,0:T(8,128)}) %reduce-scatter.2.cloned.1.call-update) | async-done | bytes 1048592 | tf_op jit(solution)/shard_map/reduce_scatter | solution.py:43
  461.2 0.0 copy-done.2
  461.2 0.0 copy-done.3
  461.2 0.0 copy-done.4
  461.2 3.4 fusion.2
  (4 shorter events, 0.0 us)
Async XLA Ops:
  7.2 2.3 copy-start
  7.2 184.6 %all-gather.6.cloned.1.call-start = ((), (), s32[]{:S(2)}) async-start(), calls=%async_computation.3 | async-start | bytes 3244032 | tf_op jit(solution)/shard_map/all_gather | solution.py:63
  7.9 295.5 %all-gather.8.cloned.1.call-start = ((), (), s32[]{:S(2)}) async-start(), calls=%async_computation.4 | async-start | bytes 3244032 | tf_op jit(solution)/shard_map/all_gather | solution.py:64
  8.7 352.7 %all-gather.4.cloned.1.call-start = ((), (), s32[]{:S(2)}) async-start(), calls=%async_computation.1 | async-start | bytes 4718592 | tf_op jit(solution)/shard_map/all_gather | solution.py:39
  9.4 451.8 %reduce-scatter.2.cloned.1.call-start = ((), (), s32[]{:S(2)}) async-start(), calls=%async_computation.2 | async-start | bytes 9437184 | tf_op jit(solution)/shard_map/reduce_scatter | solution.py:43
  17.3 1.4 copy-start.1
  310.3 151.0 %copy-start.2 = (bf16[512,512]{1,0:T(8,128)(2,1)S(1)}, bf16[512,512]{1,0:T(8,128)(2,1)}, u32[]{:S(2)}) copy-start(bf16[512,512]{1,0:T(8,128)(2,1)} %param.10) | copy-start | bytes 1572868
  310.3 151.0 %copy-start.3 = (f32[512,512]{1,0:T(8,128)S(1)}, f32[512,512]{1,0:T(8,128)}, u32[]{:S(2)}) copy-start(f32[512,512]{1,0:T(8,128)} %param.11) | copy-start | bytes 3145732
  310.3 151.0 %copy-start.4 = (f32[512,512]{1,0:T(8,128)S(1)}, f32[512,512]{1,0:T(8,128)}, u32[]{:S(2)}) copy-start(f32[512,512]{1,0:T(8,128)} %param.12) | copy-start | bytes 3145732
Sparse Core Ops, SparseCore 0:
  9.7 153.0 all-gather.5
  164.6 138.7 all-gather.7
  305.3 56.0 all-gather.3
  363.7 97.4 reduce-scatter.1
where the time goes:
time: 471 us
  waiting for transfers between devices  258 us (55%)
  blocking collectives  173 us (37%)
  matrix products  14.4 us (3%)
  between operations  13.8 us (3%)
  other arithmetic  9.56 us (2%)
    psum x1, blocking collectives, shards(): summed = lax.psum(slab_f, 'replica')  173 us
    all_gather x1, waiting for transfers between devices, shards(): lax.all_gather(outer_momentum, 'replica', axis=1, tiled=True)  112 us
    reduce_scatter x1, waiting for transfers between devices, shards(): lax.psum_scatter(lax.dot_general(columns, key_cotangent, (((0,), (0,)), (...  93.3 us
    all_gather x1, waiting for transfers between devices, shards(): lax.all_gather(key_weight, 'fsdp', axis=0, tiled=True)  51.1 us
  transfers between devices with their start and end apart: 4, of which 3 were waited for; matrix products, arithmetic and copies ran while one was open for 5% of the time, Pallas kernels for 0%

commit v1 on v0

--- a/solution.py
+++ b/solution.py
@@ -61,7 +61,10 @@
     slab_f = local_slab.astype(jnp.float32)
     whole_params, whole_momentum = (
         lax.all_gather(outer_params, "replica", axis=1, tiled=True),
-        lax.all_gather(outer_momentum, "replica", axis=1, tiled=True),
+        jnp.concatenate(
+            lax.all_to_all(jnp.stack([outer_momentum] * lax.axis_size("replica")), "replica", 0, 0),
+            axis=1,
+        ),
     )
     summed = lax.psum(slab_f, "replica")
     whole_outer, whole_new_momentum = outer_update(whole_params, whole_momentum, summed, replicas)

time: 471 us -> 367 us (0.78)
  waiting for transfers between devices: 258 us -> 95.1 us
  blocking collectives: 173 us -> 222 us
  starting transfers between devices: 0.15 us -> 8.81 us
    all_gather x1 -> x0, waiting for transfers between devices: 112 us -> none  [shards(): lax.all_gather(outer_momentum, 'replica', axis=1, tiled=True)]
    all_gather x1, waiting for transfers between devices: 51.1 us -> 0.01 us  [shards(): lax.all_gather(key_weight, 'fsdp', axis=0, tiled=True)]
    psum x1, blocking collectives: 173 us -> 222 us  [shards(): summed = lax.psum(slab_f, 'replica')]
    all_to_all x0 -> x1, starting transfers between devices: none -> 8.7 us  [shards(): lax.all_to_all(jnp.stack([outer_momentum] * lax.axis_size('replica')), 'r...]
  transfers between devices with their start and end apart: 4 -> 4, of which waited for: 3 -> 1; matrix products, arithmetic and copies ran while one was open for 5% -> 6% of each run, Pallas kernels for 0% -> 0%
where the time goes in v1:
time: 367 us
  blocking collectives  222 us (60%)
  waiting for transfers between devices  95.1 us (26%)
  matrix products  14.5 us (4%)
  between operations  13.8 us (4%)
  other arithmetic  9.5 us (3%)
  starting transfers between devices  8.81 us (2%)
    psum x1, blocking collectives, shards(): summed = lax.psum(slab_f, 'replica')  222 us
    reduce_scatter x1, waiting for transfers between devices, shards(): lax.psum_scatter(lax.dot_general(columns, key_cotangent, (((0,), (0,)), (...  93.7 us
    all_to_all x1, starting transfers between devices, shards(): lax.all_to_all(jnp.stack([outer_momentum] * lax.axis_size('replica')), 'r...  8.7 us
    dot_general x1, matrix products, shards(): lax.dot_general(columns, key_cotangent, (((0,), (0,)), ((), ())), preferr...  7.8 us
  transfers between devices with their start and end apart: 4, of which 1 were waited for; matrix products, arithmetic and copies ran while one was open for 6% of the time, Pallas kernels for 0%

profile of v1, /device:TPU:34, one launch (start us, length us, event | category | flops | bytes accessed | tf_op | source)
XLA Modules:
  0.0 367.0 jit_solution(8452503776067368769)
XLA Ops:
  7.2 0.0 copy-start
  7.2 0.0 all-gather.5.cloned.1.call-start
  7.2 0.7 all-gather.5.cloned.1.call-update
  7.9 0.0 all-gather.3.cloned.1.call-start
  8.0 0.7 all-gather.3.cloned.1.call-update
  8.7 0.0 reduce-scatter.2.cloned.1.call-start
  8.7 0.0 copy-done
  8.7 7.8 %fusion.5 = f32[4096,512]{1,0:T(8,128)} fusion(bf16[512,4096]{1,0:T(8,128)(2,1)} %param.8, bf16[512,512]{1,0:T(8,128)(2,1)S(1)} %copy-done), kind=kOutput, calls=%fused_computation.16 | convolution fusion | flops 2147483648 | bytes 13107200 | tf_op jit(solution)/shard_map/dot_general | solution.py:44
  16.5 0.0 reduce-scatter.2.cloned.1.call-update
  16.5 0.9 copy-done.5
  17.4 2.0 stack.2
  19.4 8.7 %all-to-all-start = ((f32[32,192,128]{2,1,0:T(8,128)}), f32[32,192,128]{2,1,0:T(8,128)}, u32[]{:S(2)}, u32[]{:S(2)}) async-start(f32[32,192,128]{2,1,0:T(8,128)} %stack.2), calls=%async_computation.1 | async-start | bytes 6291456 | tf_op jit(solution)/shard_map/all_to_all | solution.py:65
  28.1 0.0 copy-done.1
  28.1 221.7 %all-reduce.1 = f32[192,4096]{1,0:T(8,128)} all-reduce(bf16[192,4096]{1,0:T(8,128)(2,1)S(1)} %copy-done.1), channel_id=1, replica_groups=mesh['replica'=32,'fsdp'=8] {'replica'}, use_global_device_ids=true, to_apply=%region_1.0 | all-reduce | flops 786432 | bytes 4718592 | tf_op jit(solution)/shard_map/psum | solution.py:69
  249.9 0.0 all-to-all-done
  249.9 6.1 %multiply_convert_fusion = (bf16[192,4096]{1,0:T(8,128)(2,1)}, f32[192,4096]{1,0:T(8,128)S(1)}, f32[192,4096]{1,0:T(8,128)S(1)}) fusion(bf16[192,4096]{1,0:T(8,128)(2,1)S(1)} %copy-done.1, f32[192,4096]{1,0:T(8,128)} %all-gather.5.cloned.1.call-done, f32[192,4096]{1,0:T(8,128)} %all-reduce.1, f32[32,192,128]{2,1,0:T(8,128)} %all-to-all-done), kind=kLoop, calls=%fused_computation.1 | loop fusion | flops 9437184 | bytes 18874368 | tf_op jit(solution)/shard_map/convert_element_type | solution.py:74
  256.0 0.7 constant_dynamic-slice_fusion
  256.7 0.0 all-gather.3.cloned.1.call-done
  256.7 6.7 %convolution_convert_fusion = bf16[512,512]{1,0:T(8,128)(2,1)} fusion(bf16[512,4096]{1,0:T(8,128)(2,1)} %param.8, bf16[4096,512]{1,0:T(8,128)(2,1)} %all-gather.3.cloned.1.call-done), kind=kOutput, calls=%fused_computation.8 | convolution fusion | flops 2147745792 | bytes 8912896 | tf_op jit(solution)/shard_map/dot_general | solution.py:37
  263.5 93.7 %reduce-scatter.2.cloned.1.call-done = f32[512,512]{1,0:T(8,128)} async-done(((f32[4096,512]{1,0:T(8,128)}), f32[512,512]{1,0:T(8,128)}) %reduce-scatter.2.cloned.1.call-update) | async-done | bytes 1048592 | tf_op jit(solution)/shard_map/reduce_scatter | solution.py:43
  357.1 0.0 copy-done.2
  357.1 0.0 copy-done.3
  357.1 0.0 copy-done.4
  357.1 3.4 fusion.2
  (6 shorter events, 0.0 us)
Async XLA Ops:
  7.2 1.5 copy-start
  7.2 242.7 %all-gather.5.cloned.1.call-start = ((), (), s32[]{:S(2)}) async-start(), calls=%async_computation.4 | async-start | bytes 3244032 | tf_op jit(solution)/shard_map/all_gather | solution.py:63
  7.9 248.8 %all-gather.3.cloned.1.call-start = ((), (), s32[]{:S(2)}) async-start(), calls=%async_computation.2 | async-start | bytes 4718592 | tf_op jit(solution)/shard_map/all_gather | solution.py:39
  8.7 348.5 %reduce-scatter.2.cloned.1.call-start = ((), (), s32[]{:S(2)}) async-start(), calls=%async_computation.3 | async-start | bytes 9437184 | tf_op jit(solution)/shard_map/reduce_scatter | solution.py:43
  16.5 0.9 copy-start.5
  19.4 8.7 %copy-start.1 = (bf16[192,4096]{1,0:T(8,128)(2,1)S(1)}, bf16[192,4096]{1,0:T(8,128)(2,1)}, u32[]{:S(2)}) copy-start(bf16[192,4096]{1,0:T(8,128)(2,1)} %param.13) | copy-start | bytes 4718596
  19.4 230.5 %all-to-all-start = ((f32[32,192,128]{2,1,0:T(8,128)}), f32[32,192,128]{2,1,0:T(8,128)}, u32[]{:S(2)}, u32[]{:S(2)}) async-start(f32[32,192,128]{2,1,0:T(8,128)} %stack.2), calls=%async_computation.1 | async-start | bytes 6291456 | tf_op jit(solution)/shard_map/all_to_all | solution.py:65
  256.7 100.4 %copy-start.2 = (bf16[512,512]{1,0:T(8,128)(2,1)S(1)}, bf16[512,512]{1,0:T(8,128)(2,1)}, u32[]{:S(2)}) copy-start(bf16[512,512]{1,0:T(8,128)(2,1)} %param.10) | copy-start | bytes 1572868
  256.7 100.4 %copy-start.3 = (f32[512,512]{1,0:T(8,128)S(1)}, f32[512,512]{1,0:T(8,128)}, u32[]{:S(2)}) copy-start(f32[512,512]{1,0:T(8,128)} %param.11) | copy-start | bytes 3145732
  256.7 100.4 %copy-start.4 = (f32[512,512]{1,0:T(8,128)S(1)}, f32[512,512]{1,0:T(8,128)}, u32[]{:S(2)}) copy-start(f32[512,512]{1,0:T(8,128)} %param.12) | copy-start | bytes 3145732
Sparse Core Ops, SparseCore 0:
  9.7 179.7 all-gather.4
  191.4 55.7 all-gather.2
  249.7 107.3 reduce-scatter.1
